TPU v7x, 512 devices: a whole 4x8x8 slice. The times are simulated.
512 devices in a mesh: seq: 64 (over x, y, core), head: 8 (over z).
Axes of the slice: x: 4, y: 8, z: 8, core: 2. Of those that a mesh axis runs over, the one named last changes fastest.
Arguments:
- text_rows: bfloat16 [8192, 4096], P('seq', 'head'), may hold values from -6 to 6
- picture_rows: bfloat16 [2048, 4096], P('seq', 'head'), may hold values from -6 to 6
- picture_slots: int32 [2048], P('seq'), may hold values from 0 to 8191, as said below
- norm_gain: float32 [4096], replicated, may hold values from 0.1 to 1.9
- w_query: bfloat16 [4096, 4096], P('seq', 'head'), may hold values from -1 to 1
- w_key: bfloat16 [4096, 1024], P('seq', 'head'), may hold values from -1 to 1
- w_value: bfloat16 [4096, 1024], P('seq', 'head'), may hold values from -0.09375 to 0.09375
- w_out: bfloat16 [4096, 4096], P('head', 'seq'), may hold values from -0.5 to 0.5
- cache_keys: bfloat16 [4096, 1024], P('seq', 'head'), may hold values from -500 to 500
- cache_values: bfloat16 [4096, 1024], P('seq', 'head'), may hold values from -6 to 6
- recompute_rows: bfloat16 [512, 4096], P('seq', 'head'), may hold values from -6 to 6
- recompute_slots: int32 [512], P('seq'), may hold values from 0 to 4095, as said below
Outputs:
- mixed: bfloat16 [8192, 4096], P('seq', 'head')
Inputs may be any that keep to these rules, and one draw needn't show every extreme that they name: `picture_slots`: distinct stream positions, in runs of 256 consecutive positions, one run a tile; the first tile's run starts at position 4096 and the last tile's run ends at the stream's last position. `recompute_slots`: each aligned block b of 8 entries names distinct rows of cache rows b * 64 to (b + 1) * 64 - 1.
All inputs are finite; a program needn't handle non-finite values.
Results may differ from a plain program's by a relative error of at most 0.02.
Values may be sent and summed in bfloat16 or wider, within the bound.
A program may use at most 128 MiB of HBM per device.

v0:
```python
import jax
import jax.numpy as jnp
from jax import lax
from jax.sharding import PartitionSpec as P

D = 4096
HD = 128
EPSILON = 1e-05
ROPE_BASE = 1000000.0
NEG_FILL = -1e30


def rotate(values, positions):
    half = values.shape[-1] // 2
    freqs = ROPE_BASE ** (-jnp.arange(half, dtype=jnp.float32) / half)
    angles = positions[:, None] * freqs[None, :]
    cosine = jnp.cos(angles)[:, None, :]
    sine = jnp.sin(angles)[:, None, :]
    first = values[..., :half]
    second = values[..., half:]
    return jnp.concatenate(
        [first * cosine - second * sine, second * cosine + first * sine], axis=-1
    )


def scaled(rows_wide, squares, gain):
    return (rows_wide * lax.rsqrt(squares / D + EPSILON)[:, None] * gain[None, :]).astype(
        jnp.bfloat16
    )


def attend(carry, key_piece, value_piece, queries, allowed):
    best, total, accum = carry
    count = key_piece.shape[0]
    kv_local = queries.shape[0]
    keys_split = key_piece.reshape(count, kv_local, HD)
    values_split = value_piece.reshape(count, kv_local, HD)
    scores = jnp.einsum(
        "kgtd,nkd->kgtn", queries, keys_split, preferred_element_type=jnp.float32
    ) * HD ** (-0.5)
    scores = jnp.where(allowed, scores, NEG_FILL)
    fresh = jnp.maximum(best, jnp.max(scores, axis=-1))
    factor = jnp.exp(best - fresh)
    weights = jnp.where(allowed, jnp.exp(scores - fresh[..., None]), 0.0)
    total = total * factor + jnp.sum(weights, axis=-1)
    accum = accum * factor[..., None] + jnp.einsum(
        "kgtn,nkd->kgtd",
        weights.astype(jnp.bfloat16),
        values_split,
        preferred_element_type=jnp.float32,
    )
    return (fresh, total, accum)


def on_device(
    text_rows,
    picture_rows,
    picture_slots,
    norm_gain,
    w_query,
    w_key,
    w_value,
    w_out,
    cache_keys,
    cache_values,
    recompute_rows,
    recompute_slots,
):
    tok_rows = text_rows.shape[0]
    rec_count = recompute_rows.shape[0]
    cache_rows = cache_keys.shape[0]
    seq_index = lax.axis_index("seq")
    local_pos = seq_index * tok_rows + jnp.arange(tok_rows, dtype=jnp.int32)
    rows_piece = lax.all_gather(picture_rows, "seq", axis=0, tiled=True)
    slots_piece = lax.all_gather(picture_slots, "seq", axis=0, tiled=True)
    select = (slots_piece[None, :] == local_pos[:, None]).astype(jnp.bfloat16)
    placed = jnp.dot(select, rows_piece, preferred_element_type=jnp.float32)
    hits = jnp.sum(select.astype(jnp.float32), axis=1)
    added, hits = (placed, hits)
    stream = jnp.where(hits[:, None] > 0.5, added, text_rows.astype(jnp.float32)).astype(
        jnp.bfloat16
    )
    slice_width = stream.shape[1]
    gain_slice = lax.dynamic_slice_in_dim(
        norm_gain, lax.axis_index("head") * slice_width, slice_width, 0
    )
    stream_wide = stream.astype(jnp.float32)
    rec_wide = recompute_rows.astype(jnp.float32)
    stream_sq, rec_sq = lax.psum(
        (jnp.sum(stream_wide * stream_wide, axis=1), jnp.sum(rec_wide * rec_wide, axis=1)), "head"
    )
    normed, rec_normed = (
        lax.all_gather(scaled(stream_wide, stream_sq, gain_slice), "head", axis=1, tiled=True),
        lax.all_gather(scaled(rec_wide, rec_sq, gain_slice), "head", axis=1, tiled=True),
    )
    stacked = jnp.concatenate([normed, rec_normed], axis=0)
    query_cols = w_query.shape[1]
    key_cols = w_key.shape[1]
    pieces = (
        lax.all_gather(w_query, "seq", axis=0, tiled=True),
        lax.all_gather(w_key, "seq", axis=0, tiled=True),
        lax.all_gather(w_value, "seq", axis=0, tiled=True),
    )
    query_all = jnp.dot(stacked, pieces[0], preferred_element_type=jnp.float32)
    key_all = jnp.dot(stacked, pieces[1], preferred_element_type=jnp.float32)
    value_all = jnp.dot(stacked, pieces[2], preferred_element_type=jnp.float32)
    cache_total = cache_rows * lax.axis_size("seq")
    stream_pos = (cache_total + local_pos).astype(jnp.float32)
    rec_pos = recompute_slots.astype(jnp.float32)
    heads_local = query_cols // HD
    kv_local = key_cols // HD
    group = heads_local // kv_local
    rot_query = rotate(query_all[:tok_rows].reshape(tok_rows, heads_local, HD), stream_pos).astype(
        jnp.bfloat16
    )
    rot_key = (
        rotate(key_all[:tok_rows].reshape(tok_rows, kv_local, HD), stream_pos)
        .astype(jnp.bfloat16)
        .reshape(tok_rows, key_cols)
    )
    values_new = value_all[:tok_rows].astype(jnp.bfloat16)
    rot_rec_key = (
        rotate(key_all[tok_rows:].reshape(rec_count, kv_local, HD), rec_pos)
        .astype(jnp.bfloat16)
        .reshape(rec_count, key_cols)
    )
    rec_values = value_all[tok_rows:].astype(jnp.bfloat16)
    local_slots = recompute_slots - seq_index * cache_rows
    select = local_slots[:, None] == jnp.arange(cache_rows, dtype=jnp.int32)[None, :]
    replaced = jnp.any(select, axis=0)[:, None]
    select_cols = select.astype(jnp.bfloat16).T
    new_keys = jnp.dot(select_cols, rot_rec_key, preferred_element_type=jnp.float32).astype(
        jnp.bfloat16
    )
    new_values = jnp.dot(select_cols, rec_values, preferred_element_type=jnp.float32).astype(
        jnp.bfloat16
    )
    cache_k = jnp.where(replaced, new_keys, cache_keys)
    cache_v = jnp.where(replaced, new_values, cache_values)
    queries = jnp.transpose(rot_query.reshape(tok_rows, kv_local, group, HD), (1, 2, 0, 3))
    carry_start = (
        jnp.full((kv_local, group, tok_rows), NEG_FILL, jnp.float32),
        jnp.zeros((kv_local, group, tok_rows), jnp.float32),
        jnp.zeros((kv_local, group, tok_rows, HD), jnp.float32),
    )
    pieces = (
        lax.all_gather(cache_k, "seq", axis=0, tiled=True),
        lax.all_gather(cache_v, "seq", axis=0, tiled=True),
    )
    allowed = jnp.ones((tok_rows, pieces[0].shape[0]), jnp.bool_)
    carry_mid = attend(carry_start, pieces[0], pieces[1], queries, allowed)
    pieces = (
        lax.all_gather(rot_key, "seq", axis=0, tiled=True),
        lax.all_gather(values_new, "seq", axis=0, tiled=True),
    )
    key_pos = jnp.arange(pieces[0].shape[0], dtype=jnp.int32)
    allowed = key_pos[None, :] <= local_pos[:, None]
    best, total, accum = attend(carry_mid, pieces[0], pieces[1], queries, allowed)
    attended = (
        jnp.transpose(accum / total[..., None], (2, 0, 1, 3))
        .reshape(tok_rows, query_cols)
        .astype(jnp.bfloat16)
    )
    partial_out = jnp.dot(
        attended,
        lax.all_gather(w_out, "seq", axis=1, tiled=True),
        preferred_element_type=jnp.float32,
    )
    return lax.psum_scatter(
        partial_out.astype(jnp.bfloat16), "head", scatter_dimension=1, tiled=True
    )


def solution(mesh):
    return jax.shard_map(
        on_device,
        mesh=mesh,
        in_specs=(
            P("seq", "head"),
            P("seq", "head"),
            P("seq"),
            P(),
            P("seq", "head"),
            P("seq", "head"),
            P("seq", "head"),
            P("head", "seq"),
            P("seq", "head"),
            P("seq", "head"),
            P("seq", "head"),
            P("seq"),
        ),
        out_specs=P("seq", "head"),
        check_vma=False,
    )
```

profile of v0, /device:TPU:2, one launch (start us, length us, event | category | flops | bytes accessed | tf_op | source)
XLA Modules:
  0.0 877.7 jit_solution(5738790809692181335)
XLA Ops:
  6.5 0.7 all-gather.11.cloned.1.call-update
  7.3 0.0 all-gather.13.cloned.1.call-start
  7.3 1.3 dynamic-slice
  9.2 0.8 dynamic_slice.3
  10.0 0.8 dynamic-update-slice
  10.8 20.5 %all-reduce = s32[2048]{0:T(1024)S(1)} all-reduce(s32[2048]{0:T(1024)S(1)} %dynamic-update-slice), channel_id=1, replica_groups=mesh['seq'=64,'head'=8] {'seq'}, use_global_device_ids=true, to_apply=%add | all-reduce | flops 2048 | bytes 16384
  31.4 0.8 fusion.60
  32.2 0.3 convert_reduce_fusion
  32.5 64.4 %all-gather.11.cloned.1.call-done = bf16[2048,512]{1,0:T(8,128)(2,1)} async-done(((bf16[32,512]{1,0:T(8,128)(2,1)}), bf16[2048,512]{1,0:T(8,128)(2,1)}) %all-gather.11.cloned.1.call-update) | async-done | bytes 2097168 | tf_op jit(solution)/shard_map/all_gather | solution.py:74
  96.8 2.2 multiply_reduce_fusion.1
  99.0 18.1 %all-reduce.1 = (f32[128]{0:T(128)S(1)}, f32[8]{0:T(128)S(1)}) all-reduce(f32[128]{0:T(128)S(1)} %get-tuple-element.24, f32[8]{0:T(128)S(1)} %fusion.60), channel_id=1, replica_groups=mesh['seq'=64,'head'=8] {'head'}, use_global_device_ids=true, to_apply=%region_2.3 | all-reduce | flops 136 | bytes 1088 | tf_op jit(solution)/shard_map/psum | solution.py:89
  117.1 0.8 multiply_convert_fusion
  117.9 0.0 all-gather.17.cloned.1.call-start
  117.9 0.7 all-gather.17.cloned.1.call-update
  118.6 0.0 all-gather.21.cloned.1.call-start
  118.7 0.5 all-gather.21.cloned.1.call-update
  119.2 0.0 all-gather.15.cloned.1.call-start
  119.2 0.5 all-gather.15.cloned.1.call-update
  119.8 0.0 all-gather.19.cloned.1.call-start
  119.9 0.7 fusion.89
  120.6 0.1 fusion.71
  120.7 0.8 fusion.62
  121.5 24.6 %all_gather.39 = bf16[8,4096]{1,0:T(8,128)(2,1)S(1)} all-gather(bf16[8,512]{1,0:T(8,128)(2,1)S(1)} %fusion.62), channel_id=1, replica_groups=mesh['seq'=64,'head'=8] {'head'}, dimensions={1}, use_global_device_ids=true | all-gather | bytes 73728 | tf_op jit(solution)/shard_map/all_gather | solution.py:94
  146.0 10.3 %all-gather.13.cloned.1.call-done = bf16[128,4096]{1,0:T(8,128)(2,1)} async-done(((bf16[128,512]{1,0:T(8,128)(2,1)}), bf16[128,4096]{1,0:T(8,128)(2,1)}) %all-gather.13.cloned.1.call-update) | async-done | bytes 1048592 | tf_op jit(solution)/shard_map/all_gather | solution.py:93
  156.3 1.3 constant_dynamic-update-slice_fusion.1
  157.6 80.6 %all-gather.17.cloned.1.call-done = bf16[4096,128]{1,0:T(8,128)(2,1)} async-done(((bf16[64,128]{1,0:T(8,128)(2,1)}), bf16[4096,128]{1,0:T(8,128)(2,1)}) %all-gather.17.cloned.1.call-update) | async-done | bytes 1048592 | tf_op jit(solution)/shard_map/all_gather | solution.py:101
  238.2 1.7 fusion.90
  239.9 0.1 fusion.79
  240.0 1.6 fusion.33
  241.6 0.0 all-gather.19.cloned.1.call-update
  241.6 0.0 all-gather.25.cloned.1.call-start
  241.7 0.3 fusion.59
  242.0 0.7 pad_maximum_fusion
  242.7 0.0 all-gather.25.cloned.1.call-update
  242.7 0.0 all-gather.27.cloned.1.call-start
  242.8 78.3 %all-gather.21.cloned.1.call-done = bf16[4096,128]{1,0:T(8,128)(2,1)} async-done(((bf16[64,128]{1,0:T(8,128)(2,1)}), bf16[4096,128]{1,0:T(8,128)(2,1)}) %all-gather.21.cloned.1.call-update) | async-done | bytes 1048592 | tf_op jit(solution)/shard_map/all_gather | solution.py:102
  321.1 1.7 convolution_convert_fusion.1
  322.7 0.6 slice.55
  323.3 0.0 all-gather.27.cloned.1.call-update
  323.4 0.0 all-gather.23.cloned.1.call-start
  323.4 0.9 fusion.34
  324.3 0.0 all-gather.29.cloned.1.call-start
  324.4 0.5 all-gather.29.cloned.1.call-update
  324.9 0.0 reduce-scatter.2.cloned.1.call-start
  325.0 0.3 multiply_cosine_fusion.1
  325.3 0.7 iota_compare_fusion
  325.9 80.4 %all-gather.15.cloned.1.call-done = bf16[4096,512]{1,0:T(8,128)(2,1)} async-done(((bf16[64,512]{1,0:T(8,128)(2,1)}), bf16[4096,512]{1,0:T(8,128)(2,1)}) %all-gather.15.cloned.1.call-update) | async-done | bytes 4194320 | tf_op jit(solution)/shard_map/all_gather | solution.py:100
  406.3 2.9 fusion.41
  409.2 0.1 reshape.377
  409.3 0.2 fusion.88
  409.5 0.1 fusion.48
  409.6 79.5 %all-gather.19.cloned.1.call-done = bf16[4096,128]{1,0:T(8,128)(2,1)} async-done(((bf16[64,128]{1,0:T(8,128)(2,1)}), bf16[4096,128]{1,0:T(8,128)(2,1)}) %all-gather.19.cloned.1.call-update) | async-done | bytes 1048592 | tf_op jit(solution)/shard_map/all_gather | solution.py:147
  489.1 5.7 multiply_reduce_fusion
  494.8 78.2 %all-gather.25.cloned.1.call-done = bf16[8192,128]{1,0:T(8,128)(2,1)} async-done(((bf16[128,128]{1,0:T(8,128)(2,1)}), bf16[8192,128]{1,0:T(8,128)(2,1)}) %all-gather.25.cloned.1.call-update) | async-done | bytes 2097168 | tf_op jit(solution)/shard_map/all_gather | solution.py:153
  573.0 5.0 fusion
  578.0 1.5 fusion.6
  579.5 5.0 fusion.1
  584.5 72.4 %all-gather.27.cloned.1.call-done = bf16[8192,128]{1,0:T(8,128)(2,1)} async-done(((bf16[128,128]{1,0:T(8,128)(2,1)}), bf16[8192,128]{1,0:T(8,128)(2,1)}) %all-gather.27.cloned.1.call-update) | async-done | bytes 2097168 | tf_op jit(solution)/shard_map/all_gather | solution.py:154
  656.9 9.9 %fusion.3 = f32[4,128,128]{1,2,0:T(8,128)S(1)} fusion(f32[4,128,8192]{2,1,0:T(8,128)} %copy-done, f32[4,128]{1,0:T(4,128)S(1)} %get-tuple-element.18, pred[128,8192]{1,0:T(8,128)(4,1)S(1)} %iota_compare_fusion, bf16[8192,128]{1,0:T(8,128)(2,1)} %all-gather.27.cloned.1.call-done), kind=kOutput, calls=%fused_computation.6 | convolution fusion | flops 1094713344 | bytes 20187136 | tf_op jit(solution)/shard_map/kgtn,nkd->kgtd/dot_general | solution.py:46
  666.8 73.1 %all-gather.23.cloned.1.call-done = bf16[4096,128]{1,0:T(8,128)(2,1)} async-done(((bf16[64,128]{1,0:T(8,128)(2,1)}), bf16[4096,128]{1,0:T(8,128)(2,1)}) %all-gather.23.cloned.1.call-update) | async-done | bytes 1048592 | tf_op jit(solution)/shard_map/all_gather | solution.py:148
  740.0 5.4 fusion.38
  745.4 79.8 %all-gather.29.cloned.1.call-done = bf16[512,4096]{0,1:T(8,128)(2,1)} async-done(((bf16[512,64]{0,1:T(8,128)(2,1)}), bf16[512,4096]{0,1:T(8,128)(2,1)}) %all-gather.29.cloned.1.call-update) | async-done | bytes 4194320 | tf_op jit(solution)/shard_map/all_gather | solution.py:166
  825.2 4.7 convolution_convert_fusion
  829.9 41.3 %reduce-scatter.2.cloned.1.call-done = bf16[128,512]{1,0:T(8,128)(2,1)} async-done(((bf16[128,4096]{1,0:T(8,128)(2,1)}), bf16[128,512]{1,0:T(8,128)(2,1)}) %reduce-scatter.2.cloned.1.call-update) | async-done | bytes 131088 | tf_op jit(solution)/shard_map/reduce_scatter | solution.py:169
  (22 shorter events, 0.1 us)
Async XLA Ops:
  6.5 316.9 %copy-start.2 = (bf16[64,128]{1,0:T(8,128)(2,1)S(1)}, bf16[64,128]{1,0:T(8,128)(2,1)}, u32[]{:S(2)}) copy-start(bf16[64,128]{1,0:T(8,128)(2,1)} %param.21) | copy-start | bytes 49156
  6.5 90.3 %all-gather.11.cloned.1.call-start = ((), (), s32[]{:S(2)}) async-start(), calls=%async_computation.1 | async-start | bytes 2129920 | tf_op jit(solution)/shard_map/all_gather | solution.py:74
  7.3 149.1 %all-gather.13.cloned.1.call-start = ((), (), s32[]{:S(2)}) async-start(), calls=%async_computation.2 | async-start | bytes 1179648 | tf_op jit(solution)/shard_map/all_gather | solution.py:93
  117.9 120.3 %all-gather.17.cloned.1.call-start = ((), (), s32[]{:S(2)}) async-start(), calls=%async_computation.4 | async-start | bytes 1064960 | tf_op jit(solution)/shard_map/all_gather | solution.py:101
  118.6 202.4 %all-gather.21.cloned.1.call-start = ((), (), s32[]{:S(2)}) async-start(), calls=%async_computation.6 | async-start | bytes 1064960 | tf_op jit(solution)/shard_map/all_gather | solution.py:102
  119.2 287.1 %all-gather.15.cloned.1.call-start = ((), (), s32[]{:S(2)}) async-start(), calls=%async_computation.3 | async-start | bytes 4259840 | tf_op jit(solution)/shard_map/all_gather | solution.py:100
  119.8 369.3 %all-gather.19.cloned.1.call-start = ((), (), s32[]{:S(2)}) async-start(), calls=%async_computation.5 | async-start | bytes 1064960 | tf_op jit(solution)/shard_map/all_gather | solution.py:147
  241.6 331.4 %all-gather.25.cloned.1.call-start = ((), (), s32[]{:S(2)}) async-start(), calls=%async_computation.8 | async-start | bytes 2129920 | tf_op jit(solution)/shard_map/all_gather | solution.py:153
  242.7 414.2 %all-gather.27.cloned.1.call-start = ((), (), s32[]{:S(2)}) async-start(), calls=%async_computation.9 | async-start | bytes 2129920 | tf_op jit(solution)/shard_map/all_gather | solution.py:154
  323.4 416.6 %all-gather.23.cloned.1.call-start = ((), (), s32[]{:S(2)}) async-start(), calls=%async_computation.7 | async-start | bytes 1064960 | tf_op jit(solution)/shard_map/all_gather | solution.py:148
  324.3 500.9 %all-gather.29.cloned.1.call-start = ((), (), s32[]{:S(2)}) async-start(), calls=%async_computation.10 | async-start | bytes 4259840 | tf_op jit(solution)/shard_map/all_gather | solution.py:166
  324.9 546.2 %reduce-scatter.2.cloned.1.call-start = ((), (), s32[]{:S(2)}) async-start(), calls=%async_computation.11 | async-start | bytes 1179648 | tf_op jit(solution)/shard_map/reduce_scatter | solution.py:169
  573.0 5.0 copy-start.1
  578.0 6.5 copy-start
Sparse Core Ops, SparseCore 0:
  10.7 86.0 all-gather.10
  118.0 38.2 all-gather.12
  159.7 78.4 all-gather.16
  241.4 79.6 all-gather.20
  324.3 82.0 all-gather.14
  409.5 79.4 all-gather.18
  492.4 80.5 all-gather.24
  576.4 80.5 all-gather.26
  660.3 79.6 all-gather.22
  743.2 82.0 all-gather.28
  830.0 41.0 reduce-scatter.1
where the time goes:
time: 878 us
  waiting for transfers between devices  741 us (84%)
  blocking collectives  63.2 us (7%)
  matrix products  41.5 us (5%)
  between operations  14.1 us (2%)
  other arithmetic  12.1 us (1%)
    all_gather x1, waiting for transfers between devices, on_device(): lax.all_gather(w_key, 'seq', axis=0, tiled=True)  80.6 us
    all_gather x1, waiting for transfers between devices, on_device(): lax.all_gather(w_query, 'seq', axis=0, tiled=True)  80.4 us
    all_gather x1, waiting for transfers between devices, on_device(): lax.all_gather(w_out, 'seq', axis=1, tiled=True)  79.8 us
    all_gather x1, waiting for transfers between devices, on_device(): lax.all_gather(cache_k, 'seq', axis=0, tiled=True)  79.5 us
    all_gather x1, waiting for transfers between devices, on_device(): lax.all_gather(w_value, 'seq', axis=0, tiled=True)  78.3 us
    all_gather x1, waiting for transfers between devices, on_device(): lax.all_gather(rot_key, 'seq', axis=0, tiled=True)  78.2 us
    all_gather x1, waiting for transfers between devices, on_device(): lax.all_gather(cache_v, 'seq', axis=0, tiled=True)  73.1 us
    all_gather x1, waiting for transfers between devices, on_device(): lax.all_gather(values_new, 'seq', axis=0, tiled=True)  72.4 us
  transfers between devices with their start and end apart: 11, of which 11 were waited for; matrix products, arithmetic and copies ran while one was open for 6% of the time, Pallas kernels for 0%

commit v1 on v0

--- a/solution.py
+++ b/solution.py
@@ -8,6 +8,11 @@
 EPSILON = 1e-05
 ROPE_BASE = 1000000.0
 NEG_FILL = -1e30
+
+
+def gather_by_exchange(value, axis, dim):
+    copies = jnp.concatenate([value] * lax.axis_size(axis), axis=dim)
+    return lax.all_to_all(copies, axis, dim, dim, tiled=True)
 
 
 def rotate(values, positions):
@@ -99,7 +104,7 @@
     pieces = (
         lax.all_gather(w_query, "seq", axis=0, tiled=True),
         lax.all_gather(w_key, "seq", axis=0, tiled=True),
-        lax.all_gather(w_value, "seq", axis=0, tiled=True),
+        gather_by_exchange(w_value, "seq", 0),
     )
     query_all = jnp.dot(stacked, pieces[0], preferred_element_type=jnp.float32)
     key_all = jnp.dot(stacked, pieces[1], preferred_element_type=jnp.float32)

time: 878 us -> 800 us (0.911)
  waiting for transfers between devices: 741 us -> 600 us
  blocking collectives: 63.2 us -> 99.9 us
  local copies, waits for them, and re-layouts: 5.08 us -> 30.7 us
    all_gather x1 -> x0, waiting for transfers between devices: 78.3 us -> none  [on_device(): lax.all_gather(w_value, 'seq', axis=0, tiled=True)]
    all_gather x1, waiting for transfers between devices: 80.4 us -> 42.5 us  [on_device(): lax.all_gather(w_query, 'seq', axis=0, tiled=True)]
    all_to_all x0 -> x1, blocking collectives: none -> 36.7 us  [gather_by_exchange(): return lax.all_to_all(copies, axis, dim, dim, tiled=True)]
    unnamed x10 -> x77, local copies, waits for them, and re-layouts: 3.41 us -> 29 us
    all_gather x1, waiting for transfers between devices: 80.6 us -> 66 us  [on_device(): lax.all_gather(w_key, 'seq', axis=0, tiled=True)]
    all_gather x1, waiting for transfers between devices: 10.3 us -> 0.01 us  [on_device(): lax.all_gather(scaled(stream_wide, stream_sq, gain_slice), 'head', axis=1...]
  transfers between devices with their start and end apart: 11 -> 10, of which waited for: 11 -> 9; matrix products, arithmetic and copies ran while one was open for 6% -> 9% of each run, Pallas kernels for 0% -> 0%
where the time goes in v1:
time: 800 us; the launch traced here: 797 us
  waiting for transfers between devices  600 us (75%)
  blocking collectives  99.9 us (12%)
  matrix products  39.6 us (5%)
  local copies, waits for them, and re-layouts  30.7 us (4%)
  between operations  14.5 us (2%)
  other arithmetic  12.1 us (2%)
    all_gather x1, waiting for transfers between devices, on_device(): lax.all_gather(w_out, 'seq', axis=1, tiled=True)  80 us
    all_gather x1, waiting for transfers between devices, on_device(): lax.all_gather(cache_k, 'seq', axis=0, tiled=True)  79.5 us
    all_gather x1, waiting for transfers between devices, on_device(): lax.all_gather(rot_key, 'seq', axis=0, tiled=True)  78 us
    all_gather x1, waiting for transfers between devices, on_device(): lax.all_gather(cache_v, 'seq', axis=0, tiled=True)  73.1 us
    all_gather x1, waiting for transfers between devices, on_device(): lax.all_gather(values_new, 'seq', axis=0, tiled=True)  72.4 us
    all_gather x1, waiting for transfers between devices, on_device(): lax.all_gather(w_key, 'seq', axis=0, tiled=True)  66 us
    all_gather x1, waiting for transfers between devices, on_device(): rows_piece = lax.all_gather(picture_rows, 'seq', axis=0, tiled=True)  64.4 us
    all_gather x1, waiting for transfers between devices, on_device(): lax.all_gather(w_query, 'seq', axis=0, tiled=True)  42.5 us
  transfers between devices with their start and end apart: 10, of which 9 were waited for; matrix products, arithmetic and copies ran while one was open for 9% of the time, Pallas kernels for 0%

profile of v1, /device:TPU:2, one launch (start us, length us, event | category | flops | bytes accessed | tf_op | source)
XLA Modules:
  0.0 797.1 jit_solution(15894686588040318782)
XLA Ops:
  7.3 1.3 dynamic-slice
  9.2 0.8 dynamic_slice.3
  10.0 0.8 dynamic-update-slice
  10.8 20.5 %all-reduce = s32[2048]{0:T(1024)S(1)} all-reduce(s32[2048]{0:T(1024)S(1)} %dynamic-update-slice), channel_id=1, replica_groups=mesh['seq'=64,'head'=8] {'seq'}, use_global_device_ids=true, to_apply=%add | all-reduce | flops 2048 | bytes 16384
  31.4 0.8 fusion.60
  32.5 64.4 %all-gather.10.cloned.1.call-done = bf16[2048,512]{1,0:T(8,128)(2,1)} async-done(((bf16[32,512]{1,0:T(8,128)(2,1)}), bf16[2048,512]{1,0:T(8,128)(2,1)}) %all-gather.10.cloned.1.call-update) | async-done | bytes 2097168 | tf_op jit(solution)/shard_map/all_gather | solution.py:79
  96.8 2.2 multiply_reduce_fusion.1
  99.0 18.1 %all-reduce.1 = (f32[128]{0:T(128)S(1)}, f32[8]{0:T(128)S(1)}) all-reduce(f32[128]{0:T(128)S(1)} %get-tuple-element.24, f32[8]{0:T(128)S(1)} %fusion.60), channel_id=1, replica_groups=mesh['seq'=64,'head'=8] {'head'}, use_global_device_ids=true, to_apply=%region_2.3 | all-reduce | flops 136 | bytes 1088 | tf_op jit(solution)/shard_map/psum | solution.py:94
  117.1 0.8 multiply_convert_fusion
  120.0 0.7 constant_dynamic-update-slice_fusion.64
  120.7 0.7 constant_dynamic-update-slice_fusion.63
  121.4 0.7 constant_dynamic-update-slice_fusion.62
  122.2 0.7 constant_dynamic-update-slice_fusion.61
  122.9 0.7 constant_dynamic-update-slice_fusion.60
  123.6 0.7 constant_dynamic-update-slice_fusion.59
  124.3 0.7 constant_dynamic-update-slice_fusion.58
  125.1 0.7 constant_dynamic-update-slice_fusion.57
  125.8 0.7 constant_dynamic-update-slice_fusion.56
  126.5 0.7 constant_dynamic-update-slice_fusion.55
  127.2 0.7 constant_dynamic-update-slice_fusion.54
  128.0 0.7 constant_dynamic-update-slice_fusion.53
  128.7 0.7 constant_dynamic-update-slice_fusion.52
  129.4 0.7 constant_dynamic-update-slice_fusion.51
  130.1 0.7 constant_dynamic-update-slice_fusion.50
  130.9 0.7 constant_dynamic-update-slice_fusion.49
  131.6 0.7 constant_dynamic-update-slice_fusion.48
  132.3 0.7 constant_dynamic-update-slice_fusion.47
  133.0 0.7 constant_dynamic-update-slice_fusion.46
  133.8 0.7 constant_dynamic-update-slice_fusion.45
  134.5 0.7 constant_dynamic-update-slice_fusion.44
  135.2 0.7 constant_dynamic-update-slice_fusion.43
  135.9 0.7 constant_dynamic-update-slice_fusion.42
  136.7 0.7 constant_dynamic-update-slice_fusion.41
  137.4 0.7 constant_dynamic-update-slice_fusion.40
  138.1 0.7 constant_dynamic-update-slice_fusion.39
  139.6 0.7 constant_dynamic-update-slice_fusion.37
  140.3 0.7 constant_dynamic-update-slice_fusion.36
  141.0 0.7 constant_dynamic-update-slice_fusion.35
  141.7 0.7 constant_dynamic-update-slice_fusion.34
  143.9 0.7 constant_dynamic-update-slice_fusion.31
  144.6 0.7 fusion.89
  145.5 0.8 fusion.62
  146.2 24.6 %all_gather.36 = bf16[8,4096]{1,0:T(8,128)(2,1)S(1)} all-gather(bf16[8,512]{1,0:T(8,128)(2,1)S(1)} %fusion.62), channel_id=1, replica_groups=mesh['seq'=64,'head'=8] {'head'}, dimensions={1}, use_global_device_ids=true | all-gather | bytes 73728 | tf_op jit(solution)/shard_map/all_gather | solution.py:99
  170.8 1.3 constant_dynamic-update-slice_fusion.1
  172.1 66.0 %all-gather.16.cloned.1.call-done = bf16[4096,128]{1,0:T(8,128)(2,1)} async-done(((bf16[64,128]{1,0:T(8,128)(2,1)}), bf16[4096,128]{1,0:T(8,128)(2,1)}) %all-gather.16.cloned.1.call-update) | async-done | bytes 1048592 | tf_op jit(solution)/shard_map/all_gather | solution.py:106
  238.2 1.7 fusion.90
  240.0 0.9 fusion.33
  242.4 36.7 %all_to_all.12 = bf16[64,64,128]{2,1,0:T(8,128)(2,1)S(1)} all-to-all(bf16[64,64,128]{2,1,0:T(8,128)(2,1)S(1)} %bitcast.59), channel_id=1, replica_groups=mesh['seq'=64,'head'=8] {'seq'}, dimensions={0} | all-to-all | bytes 2097152 | tf_op jit(solution)/shard_map/all_to_all | solution.py:15
  280.3 0.9 fusion.34
  282.9 42.5 %all-gather.14.cloned.1.call-done = bf16[4096,512]{1,0:T(8,128)(2,1)} async-done(((bf16[64,512]{1,0:T(8,128)(2,1)}), bf16[4096,512]{1,0:T(8,128)(2,1)}) %all-gather.14.cloned.1.call-update) | async-done | bytes 4194320 | tf_op jit(solution)/shard_map/all_gather | solution.py:105
  325.4 2.9 fusion.41
  328.7 79.5 %all-gather.18.cloned.1.call-done = bf16[4096,128]{1,0:T(8,128)(2,1)} async-done(((bf16[64,128]{1,0:T(8,128)(2,1)}), bf16[4096,128]{1,0:T(8,128)(2,1)}) %all-gather.18.cloned.1.call-update) | async-done | bytes 1048592 | tf_op jit(solution)/shard_map/all_gather | solution.py:152
  408.2 5.7 multiply_reduce_fusion
  413.9 78.0 %all-gather.22.cloned.1.call-done = bf16[8192,128]{1,0:T(8,128)(2,1)} async-done(((bf16[128,128]{1,0:T(8,128)(2,1)}), bf16[8192,128]{1,0:T(8,128)(2,1)}) %all-gather.22.cloned.1.call-update) | async-done | bytes 2097168 | tf_op jit(solution)/shard_map/all_gather | solution.py:158
  492.0 5.0 fusion
  497.0 1.5 fusion.6
  498.5 5.0 fusion.1
  503.5 72.4 %all-gather.24.cloned.1.call-done = bf16[8192,128]{1,0:T(8,128)(2,1)} async-done(((bf16[128,128]{1,0:T(8,128)(2,1)}), bf16[8192,128]{1,0:T(8,128)(2,1)}) %all-gather.24.cloned.1.call-update) | async-done | bytes 2097168 | tf_op jit(solution)/shard_map/all_gather | solution.py:159
  575.9 9.9 %fusion.3 = f32[4,128,128]{1,2,0:T(8,128)S(1)} fusion(f32[4,128,8192]{2,1,0:T(8,128)} %copy-done, f32[4,128]{1,0:T(4,128)S(1)} %get-tuple-element.18, pred[128,8192]{1,0:T(8,128)(4,1)S(1)} %iota_compare_fusion, bf16[8192,128]{1,0:T(8,128)(2,1)} %all-gather.24.cloned.1.call-done), kind=kOutput, calls=%fused_computation.6 | convolution fusion | flops 1094713344 | bytes 20187136 | tf_op jit(solution)/shard_map/kgtn,nkd->kgtd/dot_general | solution.py:51
  585.8 73.1 %all-gather.20.cloned.1.call-done = bf16[4096,128]{1,0:T(8,128)(2,1)} async-done(((bf16[64,128]{1,0:T(8,128)(2,1)}), bf16[4096,128]{1,0:T(8,128)(2,1)}) %all-gather.20.cloned.1.call-update) | async-done | bytes 1048592 | tf_op jit(solution)/shard_map/all_gather | solution.py:153
  658.9 5.4 fusion.38
  664.3 80.0 %all-gather.26.cloned.1.call-done = bf16[512,4096]{0,1:T(8,128)(2,1)} async-done(((bf16[512,64]{0,1:T(8,128)(2,1)}), bf16[512,4096]{0,1:T(8,128)(2,1)}) %all-gather.26.cloned.1.call-update) | async-done | bytes 4194320 | tf_op jit(solution)/shard_map/all_gather | solution.py:171
  744.3 4.7 convolution_convert_fusion
  749.0 41.2 %reduce-scatter.2.cloned.1.call-done = bf16[128,512]{1,0:T(8,128)(2,1)} async-done(((bf16[128,4096]{1,0:T(8,128)(2,1)}), bf16[128,512]{1,0:T(8,128)(2,1)}) %reduce-scatter.2.cloned.1.call-update) | async-done | bytes 131088 | tf_op jit(solution)/shard_map/reduce_scatter | solution.py:174
  (88 shorter events, 10.2 us)
Async XLA Ops:
  6.5 234.4 %copy-start.2 = (bf16[64,128]{1,0:T(8,128)(2,1)S(1)}, bf16[64,128]{1,0:T(8,128)(2,1)}, u32[]{:S(2)}) copy-start(bf16[64,128]{1,0:T(8,128)(2,1)} %param.18) | copy-start | bytes 49156
  6.5 233.4 %copy-start.3 = (bf16[64,128]{1,0:T(8,128)(2,1)S(1)}, bf16[64,128]{1,0:T(8,128)(2,1)}, u32[]{:S(2)}) copy-start(bf16[64,128]{1,0:T(8,128)(2,1)} %param.20) | copy-start | bytes 49156
  6.5 273.7 %copy-start.4 = (bf16[64,128]{1,0:T(8,128)(2,1)S(1)}, bf16[64,128]{1,0:T(8,128)(2,1)}, u32[]{:S(2)}) copy-start(bf16[64,128]{1,0:T(8,128)(2,1)} %param.21) | copy-start | bytes 49156
  6.5 90.3 %all-gather.10.cloned.1.call-start = ((), (), s32[]{:S(2)}) async-start(), calls=%async_computation.2 | async-start | bytes 2129920 | tf_op jit(solution)/shard_map/all_gather | solution.py:79
  7.3 163.5 %all-gather.12.cloned.1.call-start = ((), (), s32[]{:S(2)}) async-start(), calls=%async_computation.3 | async-start | bytes 1179648 | tf_op jit(solution)/shard_map/all_gather | solution.py:98
  117.9 120.3 %all-gather.16.cloned.1.call-start = ((), (), s32[]{:S(2)}) async-start(), calls=%async_computation.5 | async-start | bytes 1064960 | tf_op jit(solution)/shard_map/all_gather | solution.py:106
  118.6 206.8 %all-gather.14.cloned.1.call-start = ((), (), s32[]{:S(2)}) async-start(), calls=%async_computation.4 | async-start | bytes 4259840 | tf_op jit(solution)/shard_map/all_gather | solution.py:105
  119.2 289.0 %all-gather.18.cloned.1.call-start = ((), (), s32[]{:S(2)}) async-start(), calls=%async_computation.6 | async-start | bytes 1064960 | tf_op jit(solution)/shard_map/all_gather | solution.py:152
  240.9 251.1 %all-gather.22.cloned.1.call-start = ((), (), s32[]{:S(2)}) async-start(), calls=%async_computation.8 | async-start | bytes 2129920 | tf_op jit(solution)/shard_map/all_gather | solution.py:158
  242.2 333.7 %all-gather.24.cloned.1.call-start = ((), (), s32[]{:S(2)}) async-start(), calls=%async_computation.9 | async-start | bytes 2129920 | tf_op jit(solution)/shard_map/all_gather | solution.py:159
  280.2 378.7 %all-gather.20.cloned.1.call-start = ((), (), s32[]{:S(2)}) async-start(), calls=%async_computation.7 | async-start | bytes 1064960 | tf_op jit(solution)/shard_map/all_gather | solution.py:153
  281.2 463.1 %all-gather.26.cloned.1.call-start = ((), (), s32[]{:S(2)}) async-start(), calls=%async_computation.10 | async-start | bytes 4259840 | tf_op jit(solution)/shard_map/all_gather | solution.py:171
  281.9 508.3 %reduce-scatter.2.cloned.1.call-start = ((), (), s32[]{:S(2)}) async-start(), calls=%async_computation.11 | async-start | bytes 1179648 | tf_op jit(solution)/shard_map/reduce_scatter | solution.py:174
  492.0 5.0 copy-start.1
  496.9 6.5 copy-start
Sparse Core Ops, SparseCore 0:
  10.7 86.0 all-gather.9
  118.0 38.0 all-gather.11
  159.5 78.6 all-gather.15
  241.4 84.0 all-gather.13
  328.6 79.4 all-gather.17
  411.4 80.5 all-gather.21
  495.3 80.5 all-gather.23
  579.2 79.6 all-gather.19
  662.3 82.0 all-gather.25
  749.1 41.0 reduce-scatter.1
